TPU v7x, 256 devices: a whole 4x4x8 slice. The times are simulated.
256 devices in a mesh: row: 16 (over x, z_hi), col: 8 (over y, core), seq: 2 (over z_lo).
Axes of the slice: x: 4, y: 4, z: 8 (z_hi: 4, z_lo: 2; z = z_hi * 2 + z_lo), core: 2. Of those that a mesh axis runs over, the one named last changes fastest.
Arguments:
- out_grads: bfloat16 [1, 2048, 32768], P(None, 'seq', 'row'), may hold values from -0.125 to 0.125
- layer_inputs: bfloat16 [1, 2048, 8192], P(None, 'seq', 'col'), may hold values from -6 to 6
- row_bits: int32 [32768], P('row'), may hold values from 0 to 1
- col_bits: int32 [8192], P('col'), may hold values from 0 to 1
- row_blocks: int32 [16], replicated, may hold values from 0 to 511
- col_blocks: int32 [8], replicated, may hold values from 0 to 63
Outputs:
- sketch: float32 [1, 1024, 1024], P(None, 'row', 'col')
Inputs may be any that keep to these rules, and one draw needn't show every extreme that they name: `row_blocks`: blocks may repeat. `col_blocks`: blocks may repeat.
All inputs are finite; a program needn't handle non-finite values.
Results may differ from a plain program's by a relative error of at most 0.0003.
Values sent between devices are 32-bit elements; how exact they have to be, the bound alone decides.
A program may use at most 64 MiB of HBM per device.

v0:
```python
import math

import jax
import jax.numpy as jnp
from jax import lax
from jax.sharding import PartitionSpec as P

D = 8192
FF = 28672
FFP = 32768
BR = 64
KR = 16
BC = 128
KC = 8


def parity_sign(first, second):
    joined = jnp.bitwise_and(first, second)
    parity = jnp.zeros(joined.shape, jnp.int32)
    for position in range(16):
        parity = parity + jnp.bitwise_and(jnp.right_shift(joined, position), 1)
    return (1 - 2 * (parity % 2)).astype(jnp.float32)


def hadamard_table(order):
    index = jnp.arange(order, dtype=jnp.int32)
    return parity_sign(index[:, None], index[None, :])


def mix_last(values):
    length = values.shape[-1]
    batch = math.prod(values.shape[:-1])
    mixing = values
    before = 1
    remaining = length
    while remaining > 1:
        factor = min(64, remaining)
        after = remaining // factor
        table = hadamard_table(factor)
        mixing = jnp.einsum(
            "ij,bpjq->bpiq",
            table,
            mixing.reshape(batch, before, factor, after),
            precision=lax.Precision.HIGHEST,
        )
        before = before * factor
        remaining = after
    return mixing.reshape(values.shape)


def mix_first(values):
    length = values.shape[0]
    width = values.shape[1]
    mixing = values
    before = 1
    remaining = length
    while remaining > 1:
        factor = min(64, remaining)
        after = remaining // factor
        table = hadamard_table(factor)
        mixing = jnp.einsum(
            "ij,pjr->pir",
            table,
            mixing.reshape(before, factor, after * width),
            precision=lax.Precision.HIGHEST,
        )
        before = before * factor
        remaining = after
    return mixing.reshape(length, width)


def body(out_grads, layer_inputs, row_bits, col_bits, row_blocks, col_blocks):
    row_local = out_grads.shape[2]
    col_local = layer_inputs.shape[2]
    row_place = lax.axis_index("row")
    col_place = lax.axis_index("col")
    global_rows = row_place * row_local + jnp.arange(row_local, dtype=jnp.int32)
    row_sign = (1 - 2 * row_bits).astype(jnp.float32) * (global_rows < FF).astype(jnp.float32)
    col_sign = (1 - 2 * col_bits).astype(jnp.float32)
    row_home = row_blocks // (row_local // BR)
    row_slot = row_blocks % (row_local // BR)
    col_home = col_blocks // (col_local // BC)
    col_slot = col_blocks % (col_local // BC)
    row_weight = parity_sign(row_home, row_place)
    col_weight = parity_sign(col_home, col_place)
    factor_scale = 1.0 / math.sqrt(FFP * D)
    grad = lax.dot_general(
        out_grads[0], layer_inputs[0], (((0,), (0,)), ((), ())), preferred_element_type=jnp.float32
    )
    grad = grad * row_sign[:, None] * col_sign[None, :]
    mixed = mix_first(grad)
    kept = (
        jnp.take(mixed.reshape(row_local // BR, BR, col_local), row_slot, axis=0)
        * row_weight[:, None, None]
    )
    kept = mix_last(kept.reshape(KR * BR, col_local))
    kept = (
        jnp.take(kept.reshape(KR * BR, col_local // BC, BC), col_slot, axis=1)
        * col_weight[None, :, None]
    )
    pieces = [kept.reshape(KR * BR, KC * BC) * factor_scale]
    stacked = jnp.stack(pieces)
    partial_rows = lax.psum_scatter(stacked, "row", scatter_dimension=1, tiled=True)
    partial_both = lax.psum_scatter(partial_rows, "col", scatter_dimension=2, tiled=True)
    return lax.psum(partial_both, "seq")


def solution(mesh):
    in_specs = (P(None, "seq", "row"), P(None, "seq", "col"), P("row"), P("col"), P(), P())
    out_specs = P(None, "row", "col")
    return jax.shard_map(body, mesh=mesh, in_specs=in_specs, out_specs=out_specs, check_vma=False)
```

profile of v0, /device:TPU:1, one launch (start us, length us, event | category | flops | bytes accessed | tf_op | source)
XLA Modules:
  0.0 256.9 jit_solution(14502040661475922665)
XLA Ops:
  6.5 0.0 copy-start
  6.5 0.0 reduce-scatter.3.cloned.1.call-start
  6.5 0.8 compare_and_fusion
  7.4 0.7 fusion.70
  8.1 0.7 subtract_convert_fusion
  8.7 0.7 convert_select_fusion
  9.4 0.0 copy-done
  9.4 9.0 %multiply_multiply_fusion = f32[2048,1024]{1,0:T(8,128)} fusion(bf16[1,1024,2048]{2,1,0:T(8,128)(2,1)} %param.6, f32[1024]{0:T(1024)S(1)} %subtract_convert_fusion, f32[2048]{0:T(1024)S(1)} %convert_select_fusion, bf16[1,1024,1024]{2,1,0:T(8,128)(2,1)S(1)} %copy-done), kind=kOutput, calls=%fused_computation.2 | convolution fusion | flops 4299161600 | bytes 14692352 | tf_op jit(solution)/shard_map/dot_general | solution.py:87
  18.5 9.4 %reshape.104 = f32[64,32768]{1,0:T(8,128)} reshape(f32[2048,1024]{1,0:T(8,128)} %multiply_multiply_fusion) | data formatting | bytes 16777216 | tf_op jit(solution)/shard_map/reshape.2
  27.8 10.4 %fusion.22 = f32[32768,64]{0,1:T(8,128)S(1)} fusion(f32[64,32768]{1,0:T(8,128)} %reshape.104), kind=kOutput, calls=%fused_computation.29 | convolution fusion | flops 1610866688 | bytes 16777216 | tf_op jit(solution)/shard_map/ij,pjr->pir/dot_general | solution.py:61
  38.3 5.0 %copy.17 = f32[8,8,32,1024]{3,2,1,0:T(8,128)S(1)} copy(f32[8,8,32,1024]{3,1,2,0:T(8,128)S(1)} %bitcast.42) | data formatting | bytes 16777216
  43.3 10.9 %fusion.19 = f32[64,1024,32]{1,2,0:T(8,128)} fusion(f32[64,32,1024]{2,1,0:T(8,128)S(1)} %bitcast.43), kind=kOutput, calls=%fused_computation.28 | convolution fusion | flops 805369856 | bytes 16777216 | tf_op jit(solution)/shard_map/ij,pjr->pir/dot_general | solution.py:61
  54.2 6.1 %gather_fusion = f32[16,64,1024]{2,1,0:T(8,128)} fusion(f32[32,64,1024]{2,1,0:T(8,128)} %bitcast.44, s32[1024]{0:T(1024)S(1)} %pad_clamp_fusion.1), kind=kCustom, calls=%fused_computation | custom fusion | bytes 8388672 | tf_op jit(solution)/shard_map/jit(_take)/gather | solution.py:93
  60.3 8.1 %copy.12 = f32[16,64,1024]{1,0,2:T(8,128)} copy(f32[16,64,1024]{2,1,0:T(8,128)} %gather_fusion) | data formatting | bytes 8388608 | tf_op jit(solution)/shard_map/jit(_take)/gather | solution.py:93
  68.4 7.6 %gather.13 = f32[1024,64,16]{0,2,1:T(8,128)} reshape(f32[16,64,1024]{1,0,2:T(8,128)} %copy.12) | data formatting | bytes 8388608 | tf_op jit(solution)/shard_map/jit(_take)/gather | solution.py:93
  76.0 0.1 mul.112
  76.1 0.1 mul.113
  76.2 0.1 broadcast_in_dim.47
  76.3 0.1 broadcast_in_dim.48
  76.3 2.7 %select_multiply_fusion = f32[1024,64,16]{0,2,1:T(8,128)S(1)} fusion(f32[1024,64,16]{0,2,1:T(8,128)} %gather.13, f32[1024]{0:T(1024)S(1)} %mul.113, pred[1024]{0:T(1024)(128)(4,1)S(1)} %broadcast_in_dim.48), kind=kLoop, calls=%fused_computation.9 | loop fusion | flops 2097152 | bytes 8393728 | tf_op jit(solution)/shard_map/mul | solution.py:93
  79.1 8.1 %fusion.5 = f32[1024,64,16]{0,1,2:T(8,128)S(1)} fusion(f32[1024,64,16]{0,2,1:T(8,128)S(1)} %select_multiply_fusion), kind=kOutput, calls=%fused_computation.10 | convolution fusion | flops 805560320 | bytes 8388608 | tf_op jit(solution)/shard_map/ij,bpjq->bpiq/dot_general | solution.py:40
  87.2 0.0 copy-start.2
  87.2 6.9 %fusion.1 = f32[1024,64,16]{0,2,1:T(8,128)} fusion(f32[1024,64,16]{0,1,2:T(8,128)S(1)} %fusion.5), kind=kOutput, calls=%fused_computation.4 | convolution fusion | flops 201342464 | bytes 8388608 | tf_op jit(solution)/shard_map/ij,bpjq->bpiq/dot_general | solution.py:40
  94.1 0.0 copy-done.2
  94.1 4.9 %gather_fusion.1 = f32[8,1024,128]{1,2,0:T(8,128)} fusion(f32[1024,8,128]{0,2,1:T(8,128)} %bitcast.45, s32[1024]{0:T(1024)S(1)} %pad_clamp_fusion), kind=kCustom, calls=%fused_computation.1 | custom fusion | bytes 8388640 | tf_op jit(solution)/shard_map/jit(_take)/gather | solution.py:98
  99.1 5.4 %copy.16 = f32[1,1024,1024]{2,1,0:T(8,128)} copy(f32[1,1024,1024]{1,2,0:T(8,128)} %bitcast.46) | data formatting | bytes 8388608 | tf_op jit(solution)/shard_map/jit(_take)/gather | solution.py:98
  104.5 0.1 broadcast_bitcast_fusion
  104.6 0.1 broadcast_bitcast_fusion.1
  104.6 0.0 copy-start.1
  104.6 5.3 %multiply_multiply_fusion.1 = f32[1,1024,1024]{2,1,0:T(8,128)} fusion(f32[1,1024,1024]{2,1,0:T(8,128)} %copy.16, f32[1024]{0:T(1024)S(1)} %broadcast_bitcast_fusion, pred[1024]{0:T(1024)(128)(4,1)S(1)} %broadcast_bitcast_fusion.1), kind=kLoop, calls=%fused_computation.8 | loop fusion | flops 3145728 | bytes 8393728 | tf_op jit(solution)/shard_map/mul | solution.py:101
  109.9 0.0 reduce-scatter.3.cloned.1.call-update
  109.9 0.0 reduce-scatter.5.cloned.1.call-start
  110.0 99.6 %reduce-scatter.3.cloned.1.call-done = f32[1,64,1024]{2,1,0:T(8,128)} async-done(((f32[1,1024,1024]{2,1,0:T(8,128)}), f32[1,64,1024]{2,1,0:T(8,128)}) %reduce-scatter.3.cloned.1.call-update) | async-done | bytes 262160 | tf_op jit(solution)/shard_map/reduce_scatter | solution.py:103
  209.6 0.0 reduce-scatter.5.cloned.1.call-update
  209.6 33.1 %reduce-scatter.5.cloned.1.call-done = f32[1,64,128]{2,1,0:T(8,128)} async-done(((f32[1,64,1024]{2,1,0:T(8,128)}), f32[1,64,128]{2,1,0:T(8,128)}) %reduce-scatter.5.cloned.1.call-update) | async-done | bytes 32784 | tf_op jit(solution)/shard_map/reduce_scatter | solution.py:104
  242.7 7.3 %psum.7 = f32[1,64,128]{2,1,0:T(8,128)} all-reduce(f32[1,64,128]{2,1,0:T(8,128)} %reduce-scatter.5.cloned.1.call-done), channel_id=1, replica_groups=mesh['row'=16,'col'=8,'seq'=2] {'seq'}, use_global_device_ids=true, to_apply=%region_2.3 | all-reduce | flops 8192 | bytes 65536 | tf_op jit(solution)/shard_map/psum | solution.py:105
  250.0 0.0 copy-done.1
  (4 shorter events, 0.1 us)
Async XLA Ops:
  6.5 2.9 %copy-start = (bf16[1,1024,1024]{2,1,0:T(8,128)(2,1)S(1)}, bf16[1,1024,1024]{2,1,0:T(8,128)(2,1)}, u32[]{:S(2)}) copy-start(bf16[1,1024,1024]{2,1,0:T(8,128)(2,1)} %param.7) | copy-start | bytes 6291460
  6.5 203.1 %reduce-scatter.3.cloned.1.call-start = ((), (), s32[]{:S(2)}) async-start(), calls=%async_computation.2 | async-start | bytes 4456448 | tf_op jit(solution)/shard_map/reduce_scatter | solution.py:103
  87.2 6.9 %copy-start.2 = (s32[8]{0:T(128)S(1)}, s32[8]{0:T(128)}, u32[]{:S(2)}) copy-start(s32[8]{0:T(128)} %param.11) | copy-start | bytes 100
  104.6 145.4 %copy-start.1 = (bf16[1,1024,1024]{2,1,0:T(8,128)(2,1)S(1)}, bf16[1,1024,1024]{2,1,0:T(8,128)(2,1)}, u32[]{:S(2)}) copy-start(bf16[1,1024,1024]{2,1,0:T(8,128)(2,1)} %param.7) | copy-start | bytes 6291460
  109.9 132.8 %reduce-scatter.5.cloned.1.call-start = ((), (), s32[]{:S(2)}) async-start(), calls=%async_computation.3 | async-start | bytes 294912 | tf_op jit(solution)/shard_map/reduce_scatter | solution.py:104
Sparse Core Ops, SparseCore 0:
  110.1 99.5 reduce-scatter.2
  212.1 30.5 reduce-scatter.4
where the time goes:
time: 261 us; the launch traced here: 257 us
  waiting for transfers between devices  133 us (51%)
  local copies, waits for them, and re-layouts  47 us (18%)
  matrix products  45.3 us (17%)
  between operations  13.5 us (5%)
  other arithmetic  11 us (4%)
  blocking collectives  7.28 us (3%)
    reduce_scatter x1, waiting for transfers between devices, body(): lax.psum_scatter(stacked, 'row', scatter_dimension=1, tiled=True)  99.6 us
    reduce_scatter x1, waiting for transfers between devices, body(): lax.psum_scatter(partial_rows, 'col', scatter_dimension=2, tiled=True)  33.1 us
    gather x3, local copies, waits for them, and re-layouts, body(): jnp.take(mixed.reshape(row_local // BR, BR, col_local), row_slot, axis=0)  21.9 us
    dot_general x2, matrix products, mix_first(): jnp.einsum('ij,pjr->pir', table, mixing.reshape(before, factor, after * w...  21.3 us
    dot_general x2, matrix products, mix_last(): jnp.einsum('ij,bpjq->bpiq', table, mixing.reshape(batch, before, factor,...  15 us
    gather x2, local copies, waits for them, and re-layouts, body(): jnp.take(kept.reshape(KR * BR, col_local // BC, BC), col_slot, axis=1)  10.3 us
    another operation x1, local copies, waits for them, and re-layouts  9.37 us
    dot_general x1, matrix products, body(): lax.dot_general(out_grads[0], layer_inputs[0], (((0,), (0,)), ((), ())),...  9.01 us
  transfers between devices with their start and end apart: 2, of which 2 were waited for; matrix products, arithmetic and copies ran while one was open for 0% of the time, Pallas kernels for 0%

commit v1 on v0

v1 whole, which is shorter than its diff:
```python
import math

import jax
import jax.numpy as jnp
from jax import lax
from jax.experimental import pallas as pl
from jax.experimental.pallas import tpu as pltpu
from jax.sharding import PartitionSpec as P

D = 8192
FF = 28672
FFP = 32768
SCALE = 1.0 / math.sqrt(FFP * D)
MESH = pl.DeviceIdType.MESH
CHUNKS = 4
F32 = jnp.float32
BF16 = jnp.bfloat16


def parity(value):
    value = value ^ (value >> 4)
    value = value ^ (value >> 2)
    value = value ^ (value >> 1)
    return value & 1


def butterfly(parts):
    stride = 1
    while stride < len(parts):
        for at in range(len(parts)):
            if not at & stride:
                low, high = parts[at], parts[at + stride]
                parts[at], parts[at + stride] = low + high, low - high
        stride *= 2
    return parts


def split(value):
    high = value.astype(BF16)
    return high, (value - high.astype(F32)).astype(BF16)


def kernel(
    row_blocks, col_blocks, row_bits, col_bits, grads, inputs, out,
    xbuf, ybuf, hmat, rmix, cmix, asend, xrecv, asum, zrecv, aall,
    bsend, brecv, ball, psend, precv,
    load_x, load_y, xs, xr, zs, zr, ys, yr, b1s, b1r, b2s, b2r, b3s, b3r, ps, pr,
):
    row, col, seq = lax.axis_index("row"), lax.axis_index("col"), lax.axis_index("seq")
    x, zh = row // 4, row % 4
    y, core = col // 2, col % 2

    loads_y = []
    for half in range(2):
        start = pl.multiple_of((x * 2 + half) * 128 + zh * 32, 32)
        loads_y.append(
            pltpu.make_async_copy(inputs.at[0, pl.ds(start, 32)], ybuf.at[half], load_y.at[half])
        )
    loads_x = []
    for chunk in range(CHUNKS):
        start = pl.multiple_of(col * 128 + chunk * 32, 32)
        loads_x.append(
            pltpu.make_async_copy(grads.at[0, pl.ds(start, 32)], xbuf.at[chunk], load_x.at[chunk])
        )
    for load in loads_y + loads_x:
        load.start()

    def at_x(step):
        return {"row": ((x + step) % 4) * 4 + zh}

    def at_zh(step):
        return {"row": x * 4 + (zh + step) % 4}

    def at_col(dy, dc):
        return {"col": ((y + dy) % 4) * 2 + (core + dc) % 2}

    def at_seq(ds, dc):
        return {"seq": (seq + ds) % 2, "col": y * 2 + (core + dc) % 2}

    barrier = pltpu.get_barrier_semaphore()
    partners = [at_x(step) for step in (1, 2, 3)] + [at_zh(step) for step in (1, 2, 3)]
    partners += [at_col(dy, dc) for dy in range(4) for dc in range(2) if dy + dc]
    partners += [at_seq(1, 0), at_seq(1, 1)]
    for partner in partners:
        pl.semaphore_signal(barrier, inc=1, device_id=partner, device_id_type=MESH)

    sends = []

    def send(src, dst, send_sem, recv_sem, device):
        copy = pltpu.make_async_remote_copy(
            src_ref=src, dst_ref=dst, send_sem=send_sem, recv_sem=recv_sem,
            device_id=device, device_id_type=MESH,
        )
        copy.start()
        sends.append(copy)
        return copy

    first = lax.broadcasted_iota(jnp.int32, (256, 256), 0)
    second = lax.broadcasted_iota(jnp.int32, (256, 256), 1)
    hmat[...] = (1 - 2 * parity(first & second)).astype(F32).astype(BF16)
    place = lax.broadcasted_iota(jnp.int32, (16, 128), 0) * 128
    place = place + lax.broadcasted_iota(jnp.int32, (16, 128), 1) + row * 2048
    row_sign = jnp.where(place < FF, (1 - 2 * row_bits[...]).astype(F32), 0.0).astype(BF16)
    col_sign = (1 - 2 * col_bits[...]).astype(F32).astype(BF16)
    lane_high = lax.broadcasted_iota(jnp.int32, (16, 128), 1) // 64
    low = lane_high == 0

    for load in loads_y:
        load.wait()
    tiles = []
    for half in range(2):
        for group in range(4):
            sign = jnp.concatenate(
                [col_sign[2 * group : 2 * group + 1], col_sign[2 * group + 1 : 2 * group + 2]], axis=1
            )
            tiles.append(ybuf[half, :, group * 256 : (group + 1) * 256] * sign)
    mixed = jnp.dot(jnp.concatenate(tiles, axis=0), hmat[...], preferred_element_type=F32)
    for half in range(2):
        for tile in range(2):
            parts = butterfly([
                mixed[(half * 4 + g) * 32 : (half * 4 + g + 1) * 32, tile * 128 : (tile + 1) * 128]
                for g in range(4)
            ])
            for g in range(4):
                cmix[g * 2 + tile, half * 32 : (half + 1) * 32] = parts[g]
    for m in range(8):
        block = col_blocks[m]
        sign = (1 - 2 * parity((block // 8) & col)).astype(F32)
        kept = cmix[block % 8] * sign
        for half in range(2):
            bsend[(m // 2) * 2 + half, m % 2] = kept[half * 32 : (half + 1) * 32]

    pl.semaphore_wait(barrier, len(partners))

    b1 = []
    for dy in (2, 1, 3, 0):
        for dc in range(2):
            if dy + dc:
                j = dy * 2 + dc - 1
                target = ((y + dy) % 4) * 2 + (core + dc) % 2
                b1.append(send(bsend.at[target], brecv.at[j], b1s.at[j], b1r.at[j], at_col(dy, dc)))

    to_x = []
    for chunk in range(CHUNKS):
        loads_x[chunk].wait()
        tiles = []
        for group in range(8):
            sign = jnp.concatenate(
                [row_sign[2 * group : 2 * group + 1], row_sign[2 * group + 1 : 2 * group + 2]], axis=1
            )
            tiles.append(xbuf[chunk, :, group * 256 : (group + 1) * 256] * sign)
        mixed = jnp.dot(jnp.concatenate(tiles, axis=0), hmat[...], preferred_element_type=F32)
        for tile in range(2):
            parts = butterfly(
                [mixed[g * 32 : (g + 1) * 32, tile * 128 : (tile + 1) * 128] for g in range(8)]
            )
            for g in range(8):
                rmix[g * 2 + tile] = parts[g]
        for k in range(16):
            block = row_blocks[k]
            sign = (1 - 2 * parity((block // 32) & row)).astype(F32) * SCALE
            kept = rmix[(block % 32) // 2]
            above, below = kept[:16], kept[16:]
            straight = jnp.where(low, above, below)
            crossed = pltpu.roll(jnp.where(low, below, above), 64, 1)
            asend[chunk, k] = jnp.where((lane_high ^ (block % 2)) == 0, straight, crossed) * sign
        copies = []
        for step in (2, 1, 3):
            first_k = ((x + step) % 4) * 4
            copies.append(send(
                asend.at[chunk, pl.ds(first_k, 4)], xrecv.at[chunk, step - 1],
                xs.at[chunk, step - 1], xr.at[chunk, step - 1], at_x(step),
            ))
        to_x.append(copies)

    to_zh = []

    def reduce_x(chunk):
        for copy in to_x[chunk]:
            copy.wait_recv()
        own = asend[chunk, pl.ds(x * 4, 4)]
        asum[chunk] = (own + xrecv[chunk, 0]) + (xrecv[chunk, 1] + xrecv[chunk, 2])
        to_zh.append([
            send(asum.at[chunk, (zh + step) % 4], zrecv.at[chunk, step - 1],
                 zs.at[chunk, step - 1], zr.at[chunk, step - 1], at_zh(step))
            for step in (2, 1, 3)
        ])

    to_y = []

    def reduce_zh(chunk):
        for copy in to_zh[chunk]:
            copy.wait_recv()
        aall[y, chunk] = (asum[chunk, zh] + zrecv[chunk, 0]) + (zrecv[chunk, 1] + zrecv[chunk, 2])
        to_y.append([
            send(aall.at[y, chunk], aall.at[y, chunk], ys.at[chunk, step - 1], yr.at[chunk, step - 1],
                 at_col(step, 0))
            for step in (2, 1, 3)
        ])

    b3 = []

    def forward(j):
        block = (zh + 4 - j) % 4
        for step in (2, 1, 3):
            b3.append(send(ball.at[x, block], ball.at[x, block], b3s.at[j, step - 1], b3r.at[j, step - 1],
                           at_x(step)))

    reduce_x(0)

    for copy in b1:
        copy.wait_recv()
    total = bsend[col]
    for j in range(7):
        total = total + brecv[j]
    ball[x, zh] = total
    b2 = {
        step: send(ball.at[x, zh], ball.at[x, zh], b2s.at[step - 1], b2r.at[step - 1], at_zh(step))
        for step in (2, 1, 3)
    }
    for chunk in range(1, CHUNKS):
        reduce_x(chunk)
    forward(0)
    for step in (1, 3):
        b2[step].wait_recv()
        forward(step)
    reduce_zh(0)
    b2[2].wait_recv()
    forward(2)
    for chunk in range(1, CHUNKS):
        reduce_zh(chunk)

    for copy in b3:
        copy.wait_recv()
    for copies in to_y:
        for copy in copies:
            copy.wait_recv()
    left_high, left_low = split(aall[...].reshape(256, 128))
    halves = []
    for half in range(2):
        right = jnp.concatenate(
            [ball[:, :, m, half * 16 : (half + 1) * 16, :].reshape(256, 128) for m in range(2)], axis=1
        )
        right_high, right_low = split(right)

        def product(first, second):
            return lax.dot_general(first, second, (((0,), (0,)), ((), ())), preferred_element_type=F32)

        full = (
            product(left_high, right_high)
            + product(left_high, right_low)
            + product(left_low, right_high)
        )
        halves.append(full[half * 64 : (half + 1) * 64])
    partial = halves[0] + halves[1]
    psend[0] = partial[:, :128]
    psend[1] = partial[:, 128:]
    mine = seq * 2 + core
    last = []
    for j, (ds, dc) in enumerate(((1, 0), (1, 1), (0, 1))):
        last.append(send(psend.at[(core + dc) % 2], precv.at[mine], ps.at[j], pr.at[j], at_seq(ds, dc)))
    precv[mine] = psend[core]
    for copy in last:
        copy.wait_recv()
    out[0] = (precv[0] + precv[1]) + (precv[2] + precv[3])
    for copy in sends:
        copy.wait_send()


def body(out_grads, layer_inputs, row_bits, col_bits, row_blocks, col_blocks):
    vmem = pl.BlockSpec(memory_space=pltpu.VMEM)
    smem = pl.BlockSpec(memory_space=pltpu.SMEM)
    hbm = pl.BlockSpec(memory_space=pl.ANY)
    dma = pltpu.SemaphoreType.DMA
    return pl.pallas_call(
        kernel,
        out_shape=jax.ShapeDtypeStruct((1, 64, 128), F32),
        in_specs=[smem, smem, vmem, vmem, hbm, hbm],
        out_specs=vmem,
        scratch_shapes=[
            pltpu.VMEM((CHUNKS, 32, 2048), BF16),
            pltpu.VMEM((2, 32, 1024), BF16),
            pltpu.VMEM((256, 256), BF16),
            pltpu.VMEM((16, 32, 128), F32),
            pltpu.VMEM((8, 64, 128), F32),
            pltpu.VMEM((CHUNKS, 16, 16, 128), F32),
            pltpu.VMEM((CHUNKS, 3, 4, 16, 128), F32),
            pltpu.VMEM((CHUNKS, 4, 16, 128), F32),
            pltpu.VMEM((CHUNKS, 3, 16, 128), F32),
            pltpu.VMEM((4, CHUNKS, 16, 128), F32),
            pltpu.VMEM((8, 2, 32, 128), F32),
            pltpu.VMEM((7, 2, 32, 128), F32),
            pltpu.VMEM((4, 4, 2, 32, 128), F32),
            pltpu.VMEM((2, 64, 128), F32),
            pltpu.VMEM((4, 64, 128), F32),
            dma((CHUNKS,)),
            dma((2,)),
            dma((CHUNKS, 3)), dma((CHUNKS, 3)),
            dma((CHUNKS, 3)), dma((CHUNKS, 3)),
            dma((CHUNKS, 3)), dma((CHUNKS, 3)),
            dma((7,)), dma((7,)),
            dma((3,)), dma((3,)),
            dma((4, 3)), dma((4, 3)),
            dma((3,)), dma((3,)),
        ],
        compiler_params=pltpu.CompilerParams(collective_id=0, has_side_effects=True),
        name="sketch",
    )(
        row_blocks, col_blocks, row_bits.reshape(16, 128), col_bits.reshape(8, 128),
        out_grads, layer_inputs,
    )


def solution(mesh):
    in_specs = (P(None, "seq", "row"), P(None, "seq", "col"), P("row"), P("col"), P(), P())
    out_specs = P(None, "row", "col")
    return jax.shard_map(body, mesh=mesh, in_specs=in_specs, out_specs=out_specs, check_vma=False)
```

time: 261 us -> 34.3 us (0.13); the launches traced: 257 us -> 34.1 us
  waiting for transfers between devices: 133 us -> 0 us
  local copies, waits for them, and re-layouts: 47 us -> 1.38 us
  matrix products: 45.3 us -> 0 us
  Pallas kernels: 0 us -> 32.7 us
  between operations: 13.5 us -> 0.01 us
  other arithmetic: 11 us -> 0 us
  blocking collectives: 7.28 us -> 0 us
    reduce_scatter x2 -> x0, waiting for transfers between devices: 133 us -> none  [the longest x1 99.6 us: body(): lax.psum_scatter(stacked, 'row', scatter_dimension=1, tiled=True)]
    dot_general x5 -> x0, matrix products: 45.3 us -> none  [the longest x2 21.3 us: mix_first(): jnp.einsum('ij,pjr->pir', table, mixing.reshape(before, factor, after * w...]
    pallas_call x0 -> x1, Pallas kernels: none -> 32.7 us  [body(): pl.pallas_call(kernel, out_shape=jax.ShapeDtypeStruct((1, 64, 128), F32),...]
    gather x5 -> x0, local copies, waits for them, and re-layouts: 32.1 us -> none  [the longest x3 21.9 us: body(): jnp.take(mixed.reshape(row_local // BR, BR, col_local), row_slot, axis=0)]
    another operation x1 -> x0, local copies, waits for them, and re-layouts: 9.37 us -> none
    mul x3 -> x0, other arithmetic: 8.69 us -> none  [the longest x1 5.29 us: body(): pieces = [kept.reshape(KR * BR, KC * BC) * factor_scale]]
    psum x1 -> x0, blocking collectives: 7.28 us -> none  [body(): return lax.psum(partial_both, 'seq')]
    unnamed x7 -> x1, local copies, waits for them, and re-layouts: 5.06 us -> 1.38 us
  transfers between devices with their start and end apart: 2 -> 0, of which waited for: 2 -> 0; matrix products, arithmetic and copies ran while one was open for 0% -> 0% of each run, Pallas kernels for 0% -> 0%
where the time goes in v1:
time: 34.3 us; the launch traced here: 34.1 us
  Pallas kernels  32.7 us (95%)
  local copies, waits for them, and re-layouts  1.38 us (4%)
    pallas_call x1, Pallas kernels, body(): pl.pallas_call(kernel, out_shape=jax.ShapeDtypeStruct((1, 64, 128), F32),...  32.7 us
    unnamed x1, local copies, waits for them, and re-layouts  1.38 us

profile of v1, /device:TPU:1, one launch (start us, length us, event | category | flops | bytes accessed | tf_op | source)
XLA Modules:
  0.0 34.1 jit_solution(1391882059547497407)
XLA Ops:
  0.0 32.7 %sketch.1 = f32[1,64,128]{2,1,0:T(8,128)} custom-call(s32[16]{0:T(128)} %row_blocks.1, s32[8]{0:T(128)} %col_blocks.1, s32[16,128]{1,0:T(8,128)} %bitcast.2, s32[8,128]{1,0:T(8,128)} %bitcast.3, bf16[1,1024,2048]{2,1,0:T(8,128)(2,1)} %grads.1, bf16[1,1024,1024]{2,1,0:T(8,128)(2,1)} %inputs.1), custom_call_target="tpu_custom_call" | custom-call | tf_op jit(solution)/shard_map/sketch/pallas_call | solution.py:275
  32.7 1.4 %copy.8 = f32[1,64,128]{2,1,0:T(8,128)} copy(f32[1,64,128]{2,1,0:T(8,128)} %sketch.1) | data formatting | bytes 65536

commit v2 on v1

v2 whole, which is shorter than its diff:
```python
import math

import jax
import jax.numpy as jnp
from jax import lax
from jax.experimental import pallas as pl
from jax.experimental.pallas import tpu as pltpu
from jax.sharding import PartitionSpec as P

D = 8192
FF = 28672
FFP = 32768
SCALE = 1.0 / math.sqrt(FFP * D)
MESH = pl.DeviceIdType.MESH
CHUNKS = 4
F32 = jnp.float32
BF16 = jnp.bfloat16


def parity(value):
    value = value ^ (value >> 4)
    value = value ^ (value >> 2)
    value = value ^ (value >> 1)
    return value & 1


def butterfly(parts):
    stride = 1
    while stride < len(parts):
        for at in range(len(parts)):
            if not at & stride:
                low, high = parts[at], parts[at + stride]
                parts[at], parts[at + stride] = low + high, low - high
        stride *= 2
    return parts


def split(value):
    high = value.astype(BF16)
    return high, (value - high.astype(F32)).astype(BF16)


def kernel(
    row_blocks_in, col_blocks_in, row_bits_in, col_bits_in, grads, inputs, out,
    row_blocks, col_blocks, row_bits, col_bits,
    xbuf, ybuf, hmat, rmix, cmix, asend, xrecv, asum, zrecv, aall,
    bsend, bpair, bsum, brecv, ball, psend, precv,
    load_x, load_y, load_s, xs, xr, zs, zr, ys, yr, b1s, b1r, b2s, b2r, b3s, b3r, ps, pr,
):
    row, col, seq = lax.axis_index("row"), lax.axis_index("col"), lax.axis_index("seq")
    x, zh = row // 4, row % 4
    y, core = col // 2, col % 2

    def at_x(step):
        return {"row": ((x + step) % 4) * 4 + zh}

    def at_zh(step):
        return {"row": x * 4 + (zh + step) % 4}

    def at_col(dy, dc):
        return {"col": ((y + dy) % 4) * 2 + (core + dc) % 2}

    other_seq = {"seq": 1 - seq}
    around = [(dy, dc) for dy in (2, 1, 3, 0) for dc in range(2) if dy + dc]

    barrier = pltpu.get_barrier_semaphore()
    partners = [at_x(step) for step in (2, 1, 3)] + [at_zh(step) for step in (2, 1, 3)]
    partners += [at_col(dy, dc) for dy, dc in around] + [other_seq]
    for partner in partners:
        pl.semaphore_signal(barrier, inc=1, device_id=partner, device_id_type=MESH)

    small = [
        pltpu.make_async_copy(src, dst, load_s.at[at])
        for at, (src, dst) in enumerate((
            (row_bits_in, row_bits), (row_blocks_in, row_blocks),
            (col_bits_in, col_bits), (col_blocks_in, col_blocks),
        ))
    ]
    loads_x = []
    for chunk in range(CHUNKS):
        start = pl.multiple_of(col * 128 + chunk * 32, 32)
        loads_x.append(
            pltpu.make_async_copy(grads.at[0, pl.ds(start, 32)], xbuf.at[chunk], load_x.at[chunk])
        )
    loads_y = [
        pltpu.make_async_copy(
            inputs.at[0, pl.ds(pl.multiple_of((x * 2 + half) * 128 + chunk * 32, 32), 32)],
            ybuf.at[chunk, half], load_y.at[chunk],
        )
        for chunk in range(CHUNKS)
        for half in range(2)
    ]
    for load in small[:2] + loads_x[:1] + small[2:] + loads_y[:2] + loads_x[1:] + loads_y[2:]:
        load.start()

    def send(src, dst, send_sem, recv_sem, device):
        pltpu.make_async_remote_copy(
            src_ref=src, dst_ref=dst, send_sem=send_sem, recv_sem=recv_sem,
            device_id=device, device_id_type=MESH,
        ).start()

    def arrived(ref, sem):
        pltpu.make_async_copy(ref, ref, sem).wait()

    first = lax.broadcasted_iota(jnp.int32, (256, 256), 0)
    second = lax.broadcasted_iota(jnp.int32, (256, 256), 1)
    hmat[...] = (1 - 2 * parity(first & second)).astype(F32).astype(BF16)
    lane_high = lax.broadcasted_iota(jnp.int32, (16, 128), 1) // 64
    low = lane_high == 0
    place = lax.broadcasted_iota(jnp.int32, (16, 128), 0) * 128
    place = place + lax.broadcasted_iota(jnp.int32, (16, 128), 1) + row * 2048
    for load in small[:2]:
        load.wait()
    row_sign = jnp.where(place < FF, (1 - 2 * row_bits[...]).astype(F32), 0.0).astype(BF16)

    def mix_columns(chunk):
        arrived(ybuf.at[chunk], load_y.at[chunk])
        tiles = []
        for half in range(2):
            for group in range(4):
                sign = jnp.concatenate(
                    [col_sign[2 * group : 2 * group + 1], col_sign[2 * group + 1 : 2 * group + 2]], axis=1
                )
                tiles.append(ybuf[chunk, half, :, group * 256 : (group + 1) * 256] * sign)
        mixed = jnp.dot(jnp.concatenate(tiles, axis=0), hmat[...], preferred_element_type=F32)
        for half in range(2):
            for tile in range(2):
                parts = butterfly([
                    mixed[(half * 4 + g) * 32 : (half * 4 + g + 1) * 32, tile * 128 : (tile + 1) * 128]
                    for g in range(4)
                ])
                for g in range(4):
                    cmix[g * 2 + tile, half * 32 : (half + 1) * 32] = parts[g]
        for m in range(8):
            block = col_blocks[m]
            sign = (1 - 2 * parity((block // 8) & col)).astype(F32)
            kept = cmix[block % 8] * sign
            bsend[chunk, m % 2, m // 2] = kept.reshape(2, 32, 128)
        send(bsend.at[chunk, 1 - core], bpair.at[chunk], b1s, b1r.at[chunk], at_col(0, 1))

    def pair_columns(chunk):
        arrived(bpair.at[chunk], b1r.at[chunk])
        bsum[chunk] = bsend[chunk, core] + bpair[chunk]
        for step in (2, 1, 3):
            send(bsum.at[chunk, (y + step) % 4], brecv.at[chunk, step - 1], b2s, b2r.at[chunk], at_col(step, 0))

    def reduce_columns(chunk):
        arrived(brecv.at[chunk], b2r.at[chunk])
        ball[x, chunk] = (bsum[chunk, y] + brecv[chunk, 0]) + (brecv[chunk, 1] + brecv[chunk, 2])
        for step in (2, 1, 3):
            send(ball.at[x, chunk], ball.at[x, chunk], b3s, b3r, at_x(step))

    def mix_rows(chunk):
        loads_x[chunk].wait()
        tiles = []
        for group in range(8):
            sign = jnp.concatenate(
                [row_sign[2 * group : 2 * group + 1], row_sign[2 * group + 1 : 2 * group + 2]], axis=1
            )
            tiles.append(xbuf[chunk, :, group * 256 : (group + 1) * 256] * sign)
        mixed = jnp.dot(jnp.concatenate(tiles, axis=0), hmat[...], preferred_element_type=F32)
        for tile in range(2):
            parts = butterfly(
                [mixed[g * 32 : (g + 1) * 32, tile * 128 : (tile + 1) * 128] for g in range(8)]
            )
            for g in range(8):
                rmix[g * 2 + tile] = parts[g]
        for k in range(16):
            block = row_blocks[k]
            sign = (1 - 2 * parity((block // 32) & row)).astype(F32) * SCALE
            kept = rmix[(block % 32) // 2]
            above, below = kept[:16], kept[16:]
            straight = jnp.where(low, above, below)
            crossed = pltpu.roll(jnp.where(low, below, above), 64, 1)
            asend[chunk, k] = jnp.where((lane_high ^ (block % 2)) == 0, straight, crossed) * sign
        if chunk == 0:
            pl.semaphore_wait(barrier, len(partners))
        for step in (2, 1, 3):
            first_k = ((x + step) % 4) * 4
            send(asend.at[chunk, pl.ds(first_k, 4)], xrecv.at[chunk, step - 1], xs, xr.at[chunk], at_x(step))

    def reduce_x(chunk):
        arrived(xrecv.at[chunk], xr.at[chunk])
        own = asend[chunk, pl.ds(x * 4, 4)]
        asum[chunk] = (own + xrecv[chunk, 0]) + (xrecv[chunk, 1] + xrecv[chunk, 2])
        for step in (2, 1, 3):
            send(asum.at[chunk, (zh + step) % 4], zrecv.at[chunk, step - 1], zs, zr.at[chunk], at_zh(step))

    def reduce_zh(chunk):
        arrived(zrecv.at[chunk], zr.at[chunk])
        aall[col, chunk] = (asum[chunk, zh] + zrecv[chunk, 0]) + (zrecv[chunk, 1] + zrecv[chunk, 2])
        for dy, dc in around:
            send(aall.at[col, chunk], aall.at[col, chunk], ys, yr.at[chunk], at_col(dy, dc))

    mix_rows(0)
    for load in small[2:]:
        load.wait()
    col_sign = (1 - 2 * col_bits[...]).astype(F32).astype(BF16)
    mix_columns(0)
    for chunk in range(1, CHUNKS):
        mix_rows(chunk)
        mix_columns(chunk)
        pair_columns(chunk - 1)
    pair_columns(CHUNKS - 1)
    reduce_x(0)
    for chunk in range(1, CHUNKS):
        reduce_x(chunk)
        reduce_columns(chunk - 1)
    reduce_columns(CHUNKS - 1)
    for chunk in range(CHUNKS):
        reduce_zh(chunk)

    arrived(ball.at[pl.ds(0, 3)], b3r)

    def product(first, second):
        return lax.dot_general(first, second, (((0,), (0,)), ((), ())), preferred_element_type=F32)

    full = None
    for chunk in range(CHUNKS):
        right_high, right_low = split(jnp.concatenate(
            [ball[:, chunk, :, half * 16 : (half + 1) * 16, :].reshape(128, 128) for half in range(2)],
            axis=1,
        ))
        arrived(aall.at[pl.ds(0, 7), chunk], yr.at[chunk])
        left_high, left_low = split(aall[:, chunk].reshape(128, 128))
        term = (
            product(left_high, right_high)
            + product(left_high, right_low)
            + product(left_low, right_high)
        )
        full = term if full is None else full + term
    psend[...] = full[:64, :128] + full[64:, 128:]
    send(psend, precv, ps, pr, other_seq)
    arrived(precv, pr)
    out[0] = psend[...] + precv[...]
    arrived(asend.at[:, pl.ds(0, 12)], xs)
    arrived(asum.at[:, pl.ds(0, 3)], zs)
    arrived(aall.at[pl.ds(0, 7)], ys)
    arrived(bpair, b1s)
    arrived(brecv, b2s)
    arrived(ball.at[pl.ds(0, 3)], b3s)
    arrived(psend, ps)


def body(out_grads, layer_inputs, row_bits, col_bits, row_blocks, col_blocks):
    vmem = pl.BlockSpec(memory_space=pltpu.VMEM)
    hbm = pl.BlockSpec(memory_space=pl.ANY)
    dma = pltpu.SemaphoreType.DMA
    return pl.pallas_call(
        kernel,
        out_shape=pltpu.VMEM((1, 64, 128), F32),
        in_specs=[hbm] * 6,
        out_specs=vmem,
        scratch_shapes=[
            pltpu.SMEM((16,), jnp.int32),
            pltpu.SMEM((8,), jnp.int32),
            pltpu.VMEM((16, 128), jnp.int32),
            pltpu.VMEM((8, 128), jnp.int32),
            pltpu.VMEM((CHUNKS, 32, 2048), BF16),
            pltpu.VMEM((CHUNKS, 2, 32, 1024), BF16),
            pltpu.VMEM((256, 256), BF16),
            pltpu.VMEM((16, 32, 128), F32),
            pltpu.VMEM((8, 64, 128), F32),
            pltpu.VMEM((CHUNKS, 16, 16, 128), F32),
            pltpu.VMEM((CHUNKS, 3, 4, 16, 128), F32),
            pltpu.VMEM((CHUNKS, 4, 16, 128), F32),
            pltpu.VMEM((CHUNKS, 3, 16, 128), F32),
            pltpu.VMEM((8, CHUNKS, 16, 128), F32),
            pltpu.VMEM((CHUNKS, 2, 4, 2, 32, 128), F32),
            pltpu.VMEM((CHUNKS, 4, 2, 32, 128), F32),
            pltpu.VMEM((CHUNKS, 4, 2, 32, 128), F32),
            pltpu.VMEM((CHUNKS, 3, 2, 32, 128), F32),
            pltpu.VMEM((4, 4, 2, 32, 128), F32),
            pltpu.VMEM((64, 128), F32),
            pltpu.VMEM((64, 128), F32),
            dma((CHUNKS,)), dma((CHUNKS,)), dma((4,)),
            dma(()), dma((CHUNKS,)),
            dma(()), dma((CHUNKS,)),
            dma(()), dma((CHUNKS,)),
            dma(()), dma((CHUNKS,)),
            dma(()), dma((CHUNKS,)),
            dma(()), dma(()),
            dma(()), dma(()),
        ],
        compiler_params=pltpu.CompilerParams(collective_id=0, has_side_effects=True),
        name="sketch",
    )(
        row_blocks, col_blocks, row_bits.reshape(16, 128), col_bits.reshape(8, 128),
        out_grads, layer_inputs,
    )


def solution(mesh):
    in_specs = (P(None, "seq", "row"), P(None, "seq", "col"), P("row"), P("col"), P(), P())
    out_specs = P(None, "row", "col")
    return jax.shard_map(body, mesh=mesh, in_specs=in_specs, out_specs=out_specs, check_vma=False)
```

time: 34.3 us -> 29 us (0.85)
  Pallas kernels: 32.7 us -> 28.3 us
  local copies, waits for them, and re-layouts: 1.38 us -> 0.62 us
    pallas_call x1, Pallas kernels: 32.7 us -> 28.3 us  [body(): pl.pallas_call(kernel, out_shape=pltpu.VMEM((1, 64, 128), F32), in_specs=...]
    unnamed x1, local copies, waits for them, and re-layouts: 1.38 us -> 0.62 us
where the time goes in v2:
time: 29 us; the launch traced here: 28.9 us
  Pallas kernels  28.3 us (98%)
  local copies, waits for them, and re-layouts  0.62 us (2%)
    pallas_call x1, Pallas kernels, body(): pl.pallas_call(kernel, out_shape=pltpu.VMEM((1, 64, 128), F32), in_specs=...  28.3 us
    unnamed x1, local copies, waits for them, and re-layouts  0.62 us

profile of v2, /device:TPU:1, one launch (start us, length us, event | category | flops | bytes accessed | tf_op | source)
XLA Modules:
  0.0 28.9 jit_solution(7563357807306903682)
XLA Ops:
  0.0 28.3 %sketch.1 = f32[1,64,128]{2,1,0:T(8,128)S(1)} custom-call(s32[16]{0:T(128)} %row_blocks_in.1, s32[8]{0:T(128)} %col_blocks_in.1, s32[16,128]{1,0:T(8,128)} %bitcast.2, s32[8,128]{1,0:T(8,128)} %bitcast.3, bf16[1,1024,2048]{2,1,0:T(8,128)(2,1)} %grads.1, bf16[1,1024,1024]{2,1,0:T(8,128)(2,1)} %inputs.1), custom_call_target="tpu_custom_call" | custom-call | tf_op jit(solution)/shard_map/sketch/pallas_call | solution.py:249
  28.3 0.6 %copy.8 = f32[1,64,128]{2,1,0:T(8,128)} copy(f32[1,64,128]{2,1,0:T(8,128)S(1)} %sketch.1) | data formatting | bytes 65536

commit v3 on v2

--- a/solution.py
+++ b/solution.py
@@ -13,6 +13,7 @@
 SCALE = 1.0 / math.sqrt(FFP * D)
 MESH = pl.DeviceIdType.MESH
 CHUNKS = 4
+TURNED = 1
 F32 = jnp.float32
 BF16 = jnp.bfloat16
 
@@ -44,8 +45,10 @@
     row_blocks_in, col_blocks_in, row_bits_in, col_bits_in, grads, inputs, out,
     row_blocks, col_blocks, row_bits, col_bits,
     xbuf, ybuf, hmat, rmix, cmix, asend, xrecv, asum, zrecv, aall,
-    bsend, bpair, bsum, brecv, ball, psend, precv,
-    load_x, load_y, load_s, xs, xr, zs, zr, ys, yr, b1s, b1r, b2s, b2r, b3s, b3r, ps, pr,
+    zturn, zsum, xturn, bsend, bpair, bsum, brecv, ball, psend, precv,
+    load_x, load_y, load_s, xs, xr, zs, zr, ys, yr, zts, ztr, xts, xtr,
+    b1s, b1r, b2s, b2r, b3s, b3r, ps, pr,
+    in_x, in_zh, in_y,
 ):
     row, col, seq = lax.axis_index("row"), lax.axis_index("col"), lax.axis_index("seq")
     x, zh = row // 4, row % 4
@@ -60,14 +63,8 @@
     def at_col(dy, dc):
         return {"col": ((y + dy) % 4) * 2 + (core + dc) % 2}
 
+    steps_x = steps_y = steps_zh = (2, 1, 3)
     other_seq = {"seq": 1 - seq}
-    around = [(dy, dc) for dy in (2, 1, 3, 0) for dc in range(2) if dy + dc]
-
-    barrier = pltpu.get_barrier_semaphore()
-    partners = [at_x(step) for step in (2, 1, 3)] + [at_zh(step) for step in (2, 1, 3)]
-    partners += [at_col(dy, dc) for dy, dc in around] + [other_seq]
-    for partner in partners:
-        pl.semaphore_signal(barrier, inc=1, device_id=partner, device_id_type=MESH)
 
     small = [
         pltpu.make_async_copy(src, dst, load_s.at[at])
@@ -90,8 +87,14 @@
         for chunk in range(CHUNKS)
         for half in range(2)
     ]
-    for load in small[:2] + loads_x[:1] + small[2:] + loads_y[:2] + loads_x[1:] + loads_y[2:]:
+    for load in loads_x[:1] + small[:2] + loads_x[1:2] + small[2:] + loads_y[:2] + loads_x[2:] + loads_y[2:]:
         load.start()
+
+    barrier = pltpu.get_barrier_semaphore()
+    partners = [at_x(1), at_x(3), at_col(1, 0), at_col(3, 0), at_col(1, 1), at_col(3, 1)]
+    partners += [at_zh(1), at_zh(3), at_col(0, 1), other_seq]
+    for partner in partners:
+        pl.semaphore_signal(barrier, inc=1, device_id=partner, device_id_type=MESH)
 
     def send(src, dst, send_sem, recv_sem, device):
         pltpu.make_async_remote_copy(
@@ -111,6 +114,10 @@
     place = place + lax.broadcasted_iota(jnp.int32, (16, 128), 1) + row * 2048
     for load in small[:2]:
         load.wait()
+    row_slots = [row_blocks[k] % 32 for k in range(16)]
+    row_signs = [
+        (1 - 2 * parity((row_blocks[k] // 32) & row)).astype(F32) * SCALE for k in range(16)
+    ]
     row_sign = jnp.where(place < FF, (1 - 2 * row_bits[...]).astype(F32), 0.0).astype(BF16)
 
     def mix_columns(chunk):
@@ -132,23 +139,21 @@
                 for g in range(4):
                     cmix[g * 2 + tile, half * 32 : (half + 1) * 32] = parts[g]
         for m in range(8):
-            block = col_blocks[m]
-            sign = (1 - 2 * parity((block // 8) & col)).astype(F32)
-            kept = cmix[block % 8] * sign
+            kept = cmix[col_slots[m]] * col_signs[m]
             bsend[chunk, m % 2, m // 2] = kept.reshape(2, 32, 128)
         send(bsend.at[chunk, 1 - core], bpair.at[chunk], b1s, b1r.at[chunk], at_col(0, 1))
 
     def pair_columns(chunk):
         arrived(bpair.at[chunk], b1r.at[chunk])
         bsum[chunk] = bsend[chunk, core] + bpair[chunk]
-        for step in (2, 1, 3):
+        for step in steps_y:
             send(bsum.at[chunk, (y + step) % 4], brecv.at[chunk, step - 1], b2s, b2r.at[chunk], at_col(step, 0))
 
     def reduce_columns(chunk):
         arrived(brecv.at[chunk], b2r.at[chunk])
         ball[x, chunk] = (bsum[chunk, y] + brecv[chunk, 0]) + (brecv[chunk, 1] + brecv[chunk, 2])
-        for step in (2, 1, 3):
-            send(ball.at[x, chunk], ball.at[x, chunk], b3s, b3r, at_x(step))
+        for step in steps_x:
+            send(ball.at[x, chunk], ball.at[x, chunk], b3s, b3r.at[chunk], at_x(step))
 
     def mix_rows(chunk):
         loads_x[chunk].wait()
@@ -166,75 +171,122 @@
             for g in range(8):
                 rmix[g * 2 + tile] = parts[g]
         for k in range(16):
-            block = row_blocks[k]
-            sign = (1 - 2 * parity((block // 32) & row)).astype(F32) * SCALE
-            kept = rmix[(block % 32) // 2]
+            kept = rmix[row_slots[k] // 2]
             above, below = kept[:16], kept[16:]
             straight = jnp.where(low, above, below)
             crossed = pltpu.roll(jnp.where(low, below, above), 64, 1)
-            asend[chunk, k] = jnp.where((lane_high ^ (block % 2)) == 0, straight, crossed) * sign
-        if chunk == 0:
-            pl.semaphore_wait(barrier, len(partners))
-        for step in (2, 1, 3):
-            first_k = ((x + step) % 4) * 4
-            send(asend.at[chunk, pl.ds(first_k, 4)], xrecv.at[chunk, step - 1], xs, xr.at[chunk], at_x(step))
+            slot = k if chunk != TURNED else (k % 4) * 4 + k // 4
+            asend[chunk, slot] = jnp.where((lane_high ^ (row_slots[k] % 2)) == 0, straight, crossed) * row_signs[k]
+
+    def send_rows(chunk, steps=(2, 1, 3)):
+        for step in steps:
+            if chunk == TURNED:
+                first_k = ((zh + step) % 4) * 4
+                send(asend.at[chunk, pl.ds(first_k, 4)], zturn.at[step - 1], zts, ztr, at_zh(step))
+            else:
+                first_k = ((x + step) % 4) * 4
+                send(asend.at[chunk, pl.ds(first_k, 4)], xrecv.at[chunk, step - 1], xs, xr.at[chunk], at_x(step))
 
     def reduce_x(chunk):
         arrived(xrecv.at[chunk], xr.at[chunk])
         own = asend[chunk, pl.ds(x * 4, 4)]
         asum[chunk] = (own + xrecv[chunk, 0]) + (xrecv[chunk, 1] + xrecv[chunk, 2])
-        for step in (2, 1, 3):
+        for step in steps_zh:
             send(asum.at[chunk, (zh + step) % 4], zrecv.at[chunk, step - 1], zs, zr.at[chunk], at_zh(step))
+
+    def spread(chunk):
+        for step in steps_y:
+            for flip in range(2):
+                send(aall.at[col, chunk], aall.at[col, chunk], ys, yr.at[chunk], at_col(step, flip))
+        send(aall.at[col, chunk], aall.at[col, chunk], ys, yr.at[chunk], at_col(0, 1))
 
     def reduce_zh(chunk):
         arrived(zrecv.at[chunk], zr.at[chunk])
         aall[col, chunk] = (asum[chunk, zh] + zrecv[chunk, 0]) + (zrecv[chunk, 1] + zrecv[chunk, 2])
-        for dy, dc in around:
-            send(aall.at[col, chunk], aall.at[col, chunk], ys, yr.at[chunk], at_col(dy, dc))
+        spread(chunk)
+
+    def turned_zh():
+        arrived(zturn, ztr)
+        own = asend[TURNED, pl.ds(zh * 4, 4)]
+        zsum[...] = (own + zturn[0]) + (zturn[1] + zturn[2])
+        for step in steps_x:
+            send(zsum.at[(x + step) % 4], xturn.at[step - 1], xts, xtr, at_x(step))
+
+    def turned_x():
+        arrived(xturn, xtr)
+        aall[col, TURNED] = (zsum[x] + xturn[0]) + (xturn[1] + xturn[2])
+        spread(TURNED)
 
     mix_rows(0)
+    pl.semaphore_wait(barrier, len(partners))
+    pl.semaphore_signal(in_x, inc=1, device_id=at_x(3), device_id_type=MESH)
+    pl.semaphore_signal(in_zh, inc=1, device_id=at_zh(3), device_id_type=MESH)
+    pl.semaphore_signal(in_y, inc=1, device_id=at_col(3, 0), device_id_type=MESH)
+    send_rows(0, (1, 3))
     for load in small[2:]:
         load.wait()
     col_sign = (1 - 2 * col_bits[...]).astype(F32).astype(BF16)
+    col_slots = [col_blocks[m] % 8 for m in range(8)]
+    col_signs = [(1 - 2 * parity((col_blocks[m] // 8) & col)).astype(F32) for m in range(8)]
     mix_columns(0)
-    for chunk in range(1, CHUNKS):
-        mix_rows(chunk)
-        mix_columns(chunk)
-        pair_columns(chunk - 1)
-    pair_columns(CHUNKS - 1)
+    mix_rows(TURNED)
+    send_rows(TURNED, (1, 3))
+    pl.semaphore_wait(in_x, 1)
+    send_rows(0, (2,))
+    pl.semaphore_wait(in_zh, 1)
+    send_rows(TURNED, (2,))
+    mix_rows(2)
+    send_rows(2, steps_x)
+    pl.semaphore_wait(in_y, 1)
+    pair_columns(0)
+    mix_columns(1)
+    mix_rows(3)
+    send_rows(3, steps_x)
+    mix_columns(2)
+    pair_columns(1)
+    mix_columns(3)
+    pair_columns(2)
+    pair_columns(3)
     reduce_x(0)
-    for chunk in range(1, CHUNKS):
-        reduce_x(chunk)
-        reduce_columns(chunk - 1)
-    reduce_columns(CHUNKS - 1)
-    for chunk in range(CHUNKS):
-        reduce_zh(chunk)
-
-    arrived(ball.at[pl.ds(0, 3)], b3r)
+    reduce_x(2)
+    reduce_columns(0)
+    reduce_x(3)
+    turned_zh()
+    reduce_columns(1)
+    reduce_zh(0)
+    reduce_columns(2)
+    reduce_zh(2)
+    reduce_columns(3)
+    turned_x()
+    reduce_zh(3)
 
     def product(first, second):
-        return lax.dot_general(first, second, (((0,), (0,)), ((), ())), preferred_element_type=F32)
+        return jnp.dot(first, second, preferred_element_type=F32)
 
     full = None
-    for chunk in range(CHUNKS):
+    for chunk in (0, 2, 1, 3):
+        arrived(ball.at[pl.ds(0, 3), chunk], b3r.at[chunk])
         right_high, right_low = split(jnp.concatenate(
-            [ball[:, chunk, :, half * 16 : (half + 1) * 16, :].reshape(128, 128) for half in range(2)],
-            axis=1,
+            [ball[:, chunk, :, half * 16 : (half + 1) * 16].reshape(128, 128) for half in range(2)],
+            axis=0,
         ))
         arrived(aall.at[pl.ds(0, 7), chunk], yr.at[chunk])
-        left_high, left_low = split(aall[:, chunk].reshape(128, 128))
+        left = aall[:, chunk].reshape(128, 128).T
+        left_high, left_low = split(jnp.concatenate([left[:64], left[64:]], axis=1))
         term = (
             product(left_high, right_high)
             + product(left_high, right_low)
             + product(left_low, right_high)
         )
         full = term if full is None else full + term
-    psend[...] = full[:64, :128] + full[64:, 128:]
+    psend[...] = full
     send(psend, precv, ps, pr, other_seq)
     arrived(precv, pr)
     out[0] = psend[...] + precv[...]
-    arrived(asend.at[:, pl.ds(0, 12)], xs)
-    arrived(asum.at[:, pl.ds(0, 3)], zs)
+    arrived(asend.at[pl.ds(0, 3), pl.ds(0, 12)], xs)
+    arrived(asum.at[pl.ds(0, 3), pl.ds(0, 3)], zs)
+    arrived(zturn, zts)
+    arrived(xturn, xts)
     arrived(aall.at[pl.ds(0, 7)], ys)
     arrived(bpair, b1s)
     arrived(brecv, b2s)
@@ -266,6 +318,9 @@
             pltpu.VMEM((CHUNKS, 4, 16, 128), F32),
             pltpu.VMEM((CHUNKS, 3, 16, 128), F32),
             pltpu.VMEM((8, CHUNKS, 16, 128), F32),
+            pltpu.VMEM((3, 4, 16, 128), F32),
+            pltpu.VMEM((4, 16, 128), F32),
+            pltpu.VMEM((3, 16, 128), F32),
             pltpu.VMEM((CHUNKS, 2, 4, 2, 32, 128), F32),
             pltpu.VMEM((CHUNKS, 4, 2, 32, 128), F32),
             pltpu.VMEM((CHUNKS, 4, 2, 32, 128), F32),
@@ -277,10 +332,12 @@
             dma(()), dma((CHUNKS,)),
             dma(()), dma((CHUNKS,)),
             dma(()), dma((CHUNKS,)),
+            dma(()), dma(()), dma(()), dma(()),
+            dma(()), dma((CHUNKS,)),
             dma(()), dma((CHUNKS,)),
             dma(()), dma((CHUNKS,)),
             dma(()), dma(()),
-            dma(()), dma(()),
+            pltpu.SemaphoreType.REGULAR, pltpu.SemaphoreType.REGULAR, pltpu.SemaphoreType.REGULAR,
         ],
         compiler_params=pltpu.CompilerParams(collective_id=0, has_side_effects=True),
         name="sketch",

time: 29 us -> 28.2 us (0.972)
  Pallas kernels: 28.3 us -> 27.5 us
    pallas_call x1, Pallas kernels: 28.3 us -> 27.5 us  [body(): pl.pallas_call(kernel, out_shape=pltpu.VMEM((1, 64, 128), F32), in_specs=...]
where the time goes in v3:
time: 28.2 us; the launch traced here: 28.1 us
  Pallas kernels  27.5 us (98%)
  local copies, waits for them, and re-layouts  0.62 us (2%)
    pallas_call x1, Pallas kernels, body(): pl.pallas_call(kernel, out_shape=pltpu.VMEM((1, 64, 128), F32), in_specs=...  27.5 us
    unnamed x1, local copies, waits for them, and re-layouts  0.62 us

profile of v3, /device:TPU:1, one launch (start us, length us, event | category | flops | bytes accessed | tf_op | source)
XLA Modules:
  0.0 28.1 jit_solution(15578794902236358305)
XLA Ops:
  0.0 27.5 %sketch.1 = f32[1,64,128]{2,1,0:T(8,128)S(1)} custom-call(s32[16]{0:T(128)} %row_blocks_in.1, s32[8]{0:T(128)} %col_blocks_in.1, s32[16,128]{1,0:T(8,128)} %bitcast.2, s32[8,128]{1,0:T(8,128)} %bitcast.3, bf16[1,1024,2048]{2,1,0:T(8,128)(2,1)} %grads.1, bf16[1,1024,1024]{2,1,0:T(8,128)(2,1)} %inputs.1), custom_call_target="tpu_custom_call" | custom-call | tf_op jit(solution)/shard_map/sketch/pallas_call | solution.py:301
  27.5 0.6 %copy.8 = f32[1,64,128]{2,1,0:T(8,128)} copy(f32[1,64,128]{2,1,0:T(8,128)S(1)} %sketch.1) | data formatting | bytes 65536

commit v4 on v3

--- a/solution.py
+++ b/solution.py
@@ -48,7 +48,7 @@
     zturn, zsum, xturn, bsend, bpair, bsum, brecv, ball, psend, precv,
     load_x, load_y, load_s, xs, xr, zs, zr, ys, yr, zts, ztr, xts, xtr,
     b1s, b1r, b2s, b2r, b3s, b3r, ps, pr,
-    in_x, in_zh, in_y,
+    in_zh,
 ):
     row, col, seq = lax.axis_index("row"), lax.axis_index("col"), lax.axis_index("seq")
     x, zh = row // 4, row % 4
@@ -63,7 +63,6 @@
     def at_col(dy, dc):
         return {"col": ((y + dy) % 4) * 2 + (core + dc) % 2}
 
-    steps_x = steps_y = steps_zh = (2, 1, 3)
     other_seq = {"seq": 1 - seq}
 
     small = [
@@ -91,7 +90,8 @@
         load.start()
 
     barrier = pltpu.get_barrier_semaphore()
-    partners = [at_x(1), at_x(3), at_col(1, 0), at_col(3, 0), at_col(1, 1), at_col(3, 1)]
+    partners = [at_x(step) for step in (2, 1, 3)]
+    partners += [at_col(step, flip) for step in (2, 1, 3) for flip in range(2)]
     partners += [at_zh(1), at_zh(3), at_col(0, 1), other_seq]
     for partner in partners:
         pl.semaphore_signal(barrier, inc=1, device_id=partner, device_id_type=MESH)
@@ -146,13 +146,13 @@
     def pair_columns(chunk):
         arrived(bpair.at[chunk], b1r.at[chunk])
         bsum[chunk] = bsend[chunk, core] + bpair[chunk]
-        for step in steps_y:
+        for step in (2, 1, 3):
             send(bsum.at[chunk, (y + step) % 4], brecv.at[chunk, step - 1], b2s, b2r.at[chunk], at_col(step, 0))
 
     def reduce_columns(chunk):
         arrived(brecv.at[chunk], b2r.at[chunk])
         ball[x, chunk] = (bsum[chunk, y] + brecv[chunk, 0]) + (brecv[chunk, 1] + brecv[chunk, 2])
-        for step in steps_x:
+        for step in (2, 1, 3):
             send(ball.at[x, chunk], ball.at[x, chunk], b3s, b3r.at[chunk], at_x(step))
 
     def mix_rows(chunk):
@@ -191,11 +191,11 @@
         arrived(xrecv.at[chunk], xr.at[chunk])
         own = asend[chunk, pl.ds(x * 4, 4)]
         asum[chunk] = (own + xrecv[chunk, 0]) + (xrecv[chunk, 1] + xrecv[chunk, 2])
-        for step in steps_zh:
+        for step in (2, 1, 3):
             send(asum.at[chunk, (zh + step) % 4], zrecv.at[chunk, step - 1], zs, zr.at[chunk], at_zh(step))
 
     def spread(chunk):
-        for step in steps_y:
+        for step in (2, 1, 3):
             for flip in range(2):
                 send(aall.at[col, chunk], aall.at[col, chunk], ys, yr.at[chunk], at_col(step, flip))
         send(aall.at[col, chunk], aall.at[col, chunk], ys, yr.at[chunk], at_col(0, 1))
@@ -209,7 +209,7 @@
         arrived(zturn, ztr)
         own = asend[TURNED, pl.ds(zh * 4, 4)]
         zsum[...] = (own + zturn[0]) + (zturn[1] + zturn[2])
-        for step in steps_x:
+        for step in (2, 1, 3):
             send(zsum.at[(x + step) % 4], xturn.at[step - 1], xts, xtr, at_x(step))
 
     def turned_x():
@@ -219,10 +219,8 @@
 
     mix_rows(0)
     pl.semaphore_wait(barrier, len(partners))
-    pl.semaphore_signal(in_x, inc=1, device_id=at_x(3), device_id_type=MESH)
     pl.semaphore_signal(in_zh, inc=1, device_id=at_zh(3), device_id_type=MESH)
-    pl.semaphore_signal(in_y, inc=1, device_id=at_col(3, 0), device_id_type=MESH)
-    send_rows(0, (1, 3))
+    send_rows(0)
     for load in small[2:]:
         load.wait()
     col_sign = (1 - 2 * col_bits[...]).astype(F32).astype(BF16)
@@ -231,17 +229,14 @@
     mix_columns(0)
     mix_rows(TURNED)
     send_rows(TURNED, (1, 3))
-    pl.semaphore_wait(in_x, 1)
-    send_rows(0, (2,))
+    mix_rows(2)
+    send_rows(2)
     pl.semaphore_wait(in_zh, 1)
     send_rows(TURNED, (2,))
-    mix_rows(2)
-    send_rows(2, steps_x)
-    pl.semaphore_wait(in_y, 1)
     pair_columns(0)
     mix_columns(1)
     mix_rows(3)
-    send_rows(3, steps_x)
+    send_rows(3)
     mix_columns(2)
     pair_columns(1)
     mix_columns(3)
@@ -337,7 +332,7 @@
             dma(()), dma((CHUNKS,)),
             dma(()), dma((CHUNKS,)),
             dma(()), dma(()),
-            pltpu.SemaphoreType.REGULAR, pltpu.SemaphoreType.REGULAR, pltpu.SemaphoreType.REGULAR,
+            pltpu.SemaphoreType.REGULAR,
         ],
         compiler_params=pltpu.CompilerParams(collective_id=0, has_side_effects=True),
         name="sketch",

time: 28.2 us -> 27.7 us (0.982)
  Pallas kernels: 27.5 us -> 27 us
    pallas_call x1, Pallas kernels: 27.5 us -> 27 us  [body(): pl.pallas_call(kernel, out_shape=pltpu.VMEM((1, 64, 128), F32), in_specs=...]
where the time goes in v4:
time: 27.7 us; the launch traced here: 27.6 us
  Pallas kernels  27 us (97%)
  local copies, waits for them, and re-layouts  0.62 us (2%)
    pallas_call x1, Pallas kernels, body(): pl.pallas_call(kernel, out_shape=pltpu.VMEM((1, 64, 128), F32), in_specs=...  27 us
    unnamed x1, local copies, waits for them, and re-layouts  0.62 us

profile of v4, /device:TPU:1, one launch (start us, length us, event | category | flops | bytes accessed | tf_op | source)
XLA Modules:
  0.0 27.6 jit_solution(9300661466834772756)
XLA Ops:
  0.0 27.0 %sketch.1 = f32[1,64,128]{2,1,0:T(8,128)S(1)} custom-call(s32[16]{0:T(128)} %row_blocks_in.1, s32[8]{0:T(128)} %col_blocks_in.1, s32[16,128]{1,0:T(8,128)} %bitcast.2, s32[8,128]{1,0:T(8,128)} %bitcast.3, bf16[1,1024,2048]{2,1,0:T(8,128)(2,1)} %grads.1, bf16[1,1024,1024]{2,1,0:T(8,128)(2,1)} %inputs.1), custom_call_target="tpu_custom_call" | custom-call | tf_op jit(solution)/shard_map/sketch/pallas_call | solution.py:296
  27.0 0.6 %copy.8 = f32[1,64,128]{2,1,0:T(8,128)} copy(f32[1,64,128]{2,1,0:T(8,128)S(1)} %sketch.1) | data formatting | bytes 65536

commit v5 on v4

--- a/solution.py
+++ b/solution.py
@@ -14,6 +14,12 @@
 MESH = pl.DeviceIdType.MESH
 CHUNKS = 4
 TURNED = 1
+LAST = 3
+ROW_TILE, COL_TILE = 16 * 128 * 4, 64 * 128 * 4
+SENT = (
+    3 * 3 * 4 * ROW_TILE + 3 * 4 * ROW_TILE + 3 * 3 * ROW_TILE + 3 * ROW_TILE + CHUNKS * 7 * ROW_TILE
+    + CHUNKS * 4 * COL_TILE + CHUNKS * 3 * COL_TILE + CHUNKS * 3 * COL_TILE + COL_TILE
+)
 F32 = jnp.float32
 BF16 = jnp.bfloat16
 
@@ -46,9 +52,7 @@
     row_blocks, col_blocks, row_bits, col_bits,
     xbuf, ybuf, hmat, rmix, cmix, asend, xrecv, asum, zrecv, aall,
     zturn, zsum, xturn, bsend, bpair, bsum, brecv, ball, psend, precv,
-    load_x, load_y, load_s, xs, xr, zs, zr, ys, yr, zts, ztr, xts, xtr,
-    b1s, b1r, b2s, b2r, b3s, b3r, ps, pr,
-    in_zh,
+    load_x, load_y, load_s, sent, xr, zr, yr, b1r, b2r, b3r, pr, in_zh, sizes,
 ):
     row, col, seq = lax.axis_index("row"), lax.axis_index("col"), lax.axis_index("seq")
     x, zh = row // 4, row % 4
@@ -76,12 +80,12 @@
     for chunk in range(CHUNKS):
         start = pl.multiple_of(col * 128 + chunk * 32, 32)
         loads_x.append(
-            pltpu.make_async_copy(grads.at[0, pl.ds(start, 32)], xbuf.at[chunk], load_x.at[chunk])
+            pltpu.make_async_copy(grads.at[0, pl.ds(start, 32)], xbuf.at[chunk], load_x.at[min(chunk, 1)])
         )
     loads_y = [
         pltpu.make_async_copy(
             inputs.at[0, pl.ds(pl.multiple_of((x * 2 + half) * 128 + chunk * 32, 32), 32)],
-            ybuf.at[chunk, half], load_y.at[chunk],
+            ybuf.at[chunk, half], load_y,
         )
         for chunk in range(CHUNKS)
         for half in range(2)
@@ -96,9 +100,9 @@
     for partner in partners:
         pl.semaphore_signal(barrier, inc=1, device_id=partner, device_id_type=MESH)
 
-    def send(src, dst, send_sem, recv_sem, device):
+    def send(src, dst, recv_sem, device):
         pltpu.make_async_remote_copy(
-            src_ref=src, dst_ref=dst, send_sem=send_sem, recv_sem=recv_sem,
+            src_ref=src, dst_ref=dst, send_sem=sent, recv_sem=recv_sem,
             device_id=device, device_id_type=MESH,
         ).start()
 
@@ -121,7 +125,8 @@
     row_sign = jnp.where(place < FF, (1 - 2 * row_bits[...]).astype(F32), 0.0).astype(BF16)
 
     def mix_columns(chunk):
-        arrived(ybuf.at[chunk], load_y.at[chunk])
+        if chunk == 0:
+            arrived(ybuf, load_y)
         tiles = []
         for half in range(2):
             for group in range(4):
@@ -141,22 +146,25 @@
         for m in range(8):
             kept = cmix[col_slots[m]] * col_signs[m]
             bsend[chunk, m % 2, m // 2] = kept.reshape(2, 32, 128)
-        send(bsend.at[chunk, 1 - core], bpair.at[chunk], b1s, b1r.at[chunk], at_col(0, 1))
+        send(bsend.at[chunk, 1 - core], bpair.at[chunk], b1r.at[chunk], at_col(0, 1))
 
     def pair_columns(chunk):
         arrived(bpair.at[chunk], b1r.at[chunk])
         bsum[chunk] = bsend[chunk, core] + bpair[chunk]
         for step in (2, 1, 3):
-            send(bsum.at[chunk, (y + step) % 4], brecv.at[chunk, step - 1], b2s, b2r.at[chunk], at_col(step, 0))
+            send(bsum.at[chunk, (y + step) % 4], brecv.at[chunk, step - 1], b2r.at[chunk], at_col(step, 0))
 
     def reduce_columns(chunk):
         arrived(brecv.at[chunk], b2r.at[chunk])
         ball[x, chunk] = (bsum[chunk, y] + brecv[chunk, 0]) + (brecv[chunk, 1] + brecv[chunk, 2])
         for step in (2, 1, 3):
-            send(ball.at[x, chunk], ball.at[x, chunk], b3s, b3r.at[chunk], at_x(step))
+            send(ball.at[x, chunk], ball.at[x, chunk], b3r.at[chunk], at_x(step))
 
     def mix_rows(chunk):
-        loads_x[chunk].wait()
+        if chunk == 0:
+            arrived(xbuf.at[0], load_x.at[0])
+        if chunk == 1:
+            arrived(xbuf.at[pl.ds(1, CHUNKS - 1)], load_x.at[1])
         tiles = []
         for group in range(8):
             sign = jnp.concatenate(
@@ -182,23 +190,23 @@
         for step in steps:
             if chunk == TURNED:
                 first_k = ((zh + step) % 4) * 4
-                send(asend.at[chunk, pl.ds(first_k, 4)], zturn.at[step - 1], zts, ztr, at_zh(step))
+                send(asend.at[chunk, pl.ds(first_k, 4)], zturn.at[step - 1], zr.at[TURNED], at_zh(step))
             else:
                 first_k = ((x + step) % 4) * 4
-                send(asend.at[chunk, pl.ds(first_k, 4)], xrecv.at[chunk, step - 1], xs, xr.at[chunk], at_x(step))
+                send(asend.at[chunk, pl.ds(first_k, 4)], xrecv.at[chunk, step - 1], xr.at[chunk], at_x(step))
 
     def reduce_x(chunk):
         arrived(xrecv.at[chunk], xr.at[chunk])
         own = asend[chunk, pl.ds(x * 4, 4)]
         asum[chunk] = (own + xrecv[chunk, 0]) + (xrecv[chunk, 1] + xrecv[chunk, 2])
         for step in (2, 1, 3):
-            send(asum.at[chunk, (zh + step) % 4], zrecv.at[chunk, step - 1], zs, zr.at[chunk], at_zh(step))
+            send(asum.at[chunk, (zh + step) % 4], zrecv.at[chunk, step - 1], zr.at[chunk], at_zh(step))
 
     def spread(chunk):
         for step in (2, 1, 3):
             for flip in range(2):
-                send(aall.at[col, chunk], aall.at[col, chunk], ys, yr.at[chunk], at_col(step, flip))
-        send(aall.at[col, chunk], aall.at[col, chunk], ys, yr.at[chunk], at_col(0, 1))
+                send(aall.at[col, chunk], aall.at[col, chunk], yr.at[chunk], at_col(step, flip))
+        send(aall.at[col, chunk], aall.at[col, chunk], yr.at[chunk], at_col(0, 1))
 
     def reduce_zh(chunk):
         arrived(zrecv.at[chunk], zr.at[chunk])
@@ -206,14 +214,14 @@
         spread(chunk)
 
     def turned_zh():
-        arrived(zturn, ztr)
+        arrived(zturn, zr.at[TURNED])
         own = asend[TURNED, pl.ds(zh * 4, 4)]
         zsum[...] = (own + zturn[0]) + (zturn[1] + zturn[2])
         for step in (2, 1, 3):
-            send(zsum.at[(x + step) % 4], xturn.at[step - 1], xts, xtr, at_x(step))
+            send(zsum.at[(x + step) % 4], xturn.at[step - 1], xr.at[TURNED], at_x(step))
 
     def turned_x():
-        arrived(xturn, xtr)
+        arrived(xturn, xr.at[TURNED])
         aall[col, TURNED] = (zsum[x] + xturn[0]) + (xturn[1] + xturn[2])
         spread(TURNED)
 
@@ -268,25 +276,28 @@
         arrived(aall.at[pl.ds(0, 7), chunk], yr.at[chunk])
         left = aall[:, chunk].reshape(128, 128).T
         left_high, left_low = split(jnp.concatenate([left[:64], left[64:]], axis=1))
+        if chunk == LAST:
+            break
         term = (
             product(left_high, right_high)
             + product(left_high, right_low)
             + product(left_low, right_high)
         )
         full = term if full is None else full + term
-    psend[...] = full
-    send(psend, precv, ps, pr, other_seq)
-    arrived(precv, pr)
-    out[0] = psend[...] + precv[...]
-    arrived(asend.at[pl.ds(0, 3), pl.ds(0, 12)], xs)
-    arrived(asum.at[pl.ds(0, 3), pl.ds(0, 3)], zs)
-    arrived(zturn, zts)
-    arrived(xturn, xts)
-    arrived(aall.at[pl.ds(0, 7)], ys)
-    arrived(bpair, b1s)
-    arrived(brecv, b2s)
-    arrived(ball.at[pl.ds(0, 3)], b3s)
-    arrived(psend, ps)
+    for part in range(2):
+        rows = slice(part * 32, (part + 1) * 32)
+        term = (
+            product(left_high[rows], right_high)
+            + product(left_high[rows], right_low)
+            + product(left_low[rows], right_high)
+        )
+        psend[rows] = full[rows] + term
+        send(psend.at[rows], precv.at[rows], pr.at[part], other_seq)
+    for part in range(2):
+        rows = slice(part * 32, (part + 1) * 32)
+        arrived(precv.at[rows], pr.at[part])
+        out[0, rows] = psend[rows] + precv[rows]
+    arrived(sizes, sent)
 
 
 def body(out_grads, layer_inputs, row_bits, col_bits, row_blocks, col_blocks):
@@ -323,16 +334,12 @@
             pltpu.VMEM((4, 4, 2, 32, 128), F32),
             pltpu.VMEM((64, 128), F32),
             pltpu.VMEM((64, 128), F32),
-            dma((CHUNKS,)), dma((CHUNKS,)), dma((4,)),
-            dma(()), dma((CHUNKS,)),
-            dma(()), dma((CHUNKS,)),
-            dma(()), dma((CHUNKS,)),
-            dma(()), dma(()), dma(()), dma(()),
-            dma(()), dma((CHUNKS,)),
-            dma(()), dma((CHUNKS,)),
-            dma(()), dma((CHUNKS,)),
-            dma(()), dma(()),
+            dma((2,)), dma(()), dma((4,)), dma(()),
+            dma((CHUNKS,)), dma((CHUNKS,)), dma((CHUNKS,)),
+            dma((CHUNKS,)), dma((CHUNKS,)), dma((CHUNKS,)),
+            dma((2,)),
             pltpu.SemaphoreType.REGULAR,
+            pltpu.VMEM((SENT // 512, 128), F32),
         ],
         compiler_params=pltpu.CompilerParams(collective_id=0, has_side_effects=True),
         name="sketch",

time: 27.7 us -> 27.5 us (level)
  no operation moved by 1% of the time
where the time goes in v5:
time: 27.5 us; the launch traced here: 27.4 us
  Pallas kernels  26.8 us (97%)
  local copies, waits for them, and re-layouts  0.62 us (2%)
    pallas_call x1, Pallas kernels, body(): pl.pallas_call(kernel, out_shape=pltpu.VMEM((1, 64, 128), F32), in_specs=...  26.8 us
    unnamed x1, local copies, waits for them, and re-layouts  0.62 us

profile of v5, /device:TPU:1, one launch (start us, length us, event | category | flops | bytes accessed | tf_op | source)
XLA Modules:
  0.0 27.4 jit_solution(3021074573521460157)
XLA Ops:
  0.0 26.8 %sketch.1 = f32[1,64,128]{2,1,0:T(8,128)S(1)} custom-call(s32[16]{0:T(128)} %row_blocks_in.1, s32[8]{0:T(128)} %col_blocks_in.1, s32[16,128]{1,0:T(8,128)} %bitcast.2, s32[8,128]{1,0:T(8,128)} %bitcast.3, bf16[1,1024,2048]{2,1,0:T(8,128)(2,1)} %grads.1, bf16[1,1024,1024]{2,1,0:T(8,128)(2,1)} %inputs.1), custom_call_target="tpu_custom_call" | custom-call | tf_op jit(solution)/shard_map/sketch/pallas_call | solution.py:307
  26.8 0.6 %copy.8 = f32[1,64,128]{2,1,0:T(8,128)} copy(f32[1,64,128]{2,1,0:T(8,128)S(1)} %sketch.1) | data formatting | bytes 65536

commit v6 on v5

--- a/solution.py
+++ b/solution.py
@@ -31,6 +31,12 @@
     return value & 1
 
 
+def parity_of_four(value):
+    value = value ^ (value >> 2)
+    value = value ^ (value >> 1)
+    return value & 1
+
+
 def butterfly(parts):
     stride = 1
     while stride < len(parts):
@@ -68,6 +74,13 @@
         return {"col": ((y + dy) % 4) * 2 + (core + dc) % 2}
 
     other_seq = {"seq": 1 - seq}
+
+    barrier = pltpu.get_barrier_semaphore()
+    partners = [at_x(step) for step in (2, 1, 3)]
+    partners += [at_col(step, flip) for step in (2, 1, 3) for flip in range(2)]
+    partners += [at_zh(1), at_zh(3), at_col(0, 1), other_seq]
+    for partner in partners:
+        pl.semaphore_signal(barrier, inc=1, device_id=partner, device_id_type=MESH)
 
     small = [
         pltpu.make_async_copy(src, dst, load_s.at[at])
@@ -93,13 +106,6 @@
     for load in loads_x[:1] + small[:2] + loads_x[1:2] + small[2:] + loads_y[:2] + loads_x[2:] + loads_y[2:]:
         load.start()
 
-    barrier = pltpu.get_barrier_semaphore()
-    partners = [at_x(step) for step in (2, 1, 3)]
-    partners += [at_col(step, flip) for step in (2, 1, 3) for flip in range(2)]
-    partners += [at_zh(1), at_zh(3), at_col(0, 1), other_seq]
-    for partner in partners:
-        pl.semaphore_signal(barrier, inc=1, device_id=partner, device_id_type=MESH)
-
     def send(src, dst, recv_sem, device):
         pltpu.make_async_remote_copy(
             src_ref=src, dst_ref=dst, send_sem=sent, recv_sem=recv_sem,
@@ -116,12 +122,7 @@
     low = lane_high == 0
     place = lax.broadcasted_iota(jnp.int32, (16, 128), 0) * 128
     place = place + lax.broadcasted_iota(jnp.int32, (16, 128), 1) + row * 2048
-    for load in small[:2]:
-        load.wait()
-    row_slots = [row_blocks[k] % 32 for k in range(16)]
-    row_signs = [
-        (1 - 2 * parity((row_blocks[k] // 32) & row)).astype(F32) * SCALE for k in range(16)
-    ]
+    small[0].wait()
     row_sign = jnp.where(place < FF, (1 - 2 * row_bits[...]).astype(F32), 0.0).astype(BF16)
 
     def mix_columns(chunk):
@@ -160,9 +161,16 @@
         for step in (2, 1, 3):
             send(ball.at[x, chunk], ball.at[x, chunk], b3r.at[chunk], at_x(step))
 
+    row_slots, row_signs = [], []
+
     def mix_rows(chunk):
         if chunk == 0:
             arrived(xbuf.at[0], load_x.at[0])
+            small[1].wait()
+            row_slots.extend(row_blocks[k] % 32 for k in range(16))
+            row_signs.extend(
+                (1 - 2 * parity_of_four((row_blocks[k] // 32) & row)).astype(F32) * SCALE for k in range(16)
+            )
         if chunk == 1:
             arrived(xbuf.at[pl.ds(1, CHUNKS - 1)], load_x.at[1])
         tiles = []
@@ -233,7 +241,7 @@
         load.wait()
     col_sign = (1 - 2 * col_bits[...]).astype(F32).astype(BF16)
     col_slots = [col_blocks[m] % 8 for m in range(8)]
-    col_signs = [(1 - 2 * parity((col_blocks[m] // 8) & col)).astype(F32) for m in range(8)]
+    col_signs = [(1 - 2 * parity_of_four((col_blocks[m] // 8) & col)).astype(F32) for m in range(8)]
     mix_columns(0)
     mix_rows(TURNED)
     send_rows(TURNED, (1, 3))

time: 27.5 us -> 27.4 us (level)
  no operation moved by 1% of the time
where the time goes in v6:
time: 27.4 us; the launch traced here: 27.3 us
  Pallas kernels  26.7 us (97%)
  local copies, waits for them, and re-layouts  0.62 us (2%)
    pallas_call x1, Pallas kernels, body(): pl.pallas_call(kernel, out_shape=pltpu.VMEM((1, 64, 128), F32), in_specs=...  26.7 us
    unnamed x1, local copies, waits for them, and re-layouts  0.62 us

profile of v6, /device:TPU:1, one launch (start us, length us, event | category | flops | bytes accessed | tf_op | source)
XLA Modules:
  0.0 27.3 jit_solution(6748922736646054998)
XLA Ops:
  0.0 26.7 %sketch.1 = f32[1,64,128]{2,1,0:T(8,128)S(1)} custom-call(s32[16]{0:T(128)} %row_blocks_in.1, s32[8]{0:T(128)} %col_blocks_in.1, s32[16,128]{1,0:T(8,128)} %bitcast.2, s32[8,128]{1,0:T(8,128)} %bitcast.3, bf16[1,1024,2048]{2,1,0:T(8,128)(2,1)} %grads.1, bf16[1,1024,1024]{2,1,0:T(8,128)(2,1)} %inputs.1), custom_call_target="tpu_custom_call" | custom-call | tf_op jit(solution)/shard_map/sketch/pallas_call | solution.py:315
  26.7 0.6 %copy.8 = f32[1,64,128]{2,1,0:T(8,128)} copy(f32[1,64,128]{2,1,0:T(8,128)S(1)} %sketch.1) | data formatting | bytes 65536

commit v7 on v6

--- a/solution.py
+++ b/solution.py
@@ -264,11 +264,11 @@
     reduce_x(3)
     turned_zh()
     reduce_columns(1)
+    reduce_columns(2)
     reduce_zh(0)
-    reduce_columns(2)
     reduce_zh(2)
+    turned_x()
     reduce_columns(3)
-    turned_x()
     reduce_zh(3)
 
     def product(first, second):

time: 27.4 us -> 27.4 us (level)
  no operation moved by 1% of the time
where the time goes in v7:
time: 27.4 us; the launch traced here: 27.3 us
  Pallas kernels  26.7 us (97%)
  local copies, waits for them, and re-layouts  0.62 us (2%)
    pallas_call x1, Pallas kernels, body(): pl.pallas_call(kernel, out_shape=pltpu.VMEM((1, 64, 128), F32), in_specs=...  26.7 us
    unnamed x1, local copies, waits for them, and re-layouts  0.62 us

profile of v7, /device:TPU:1, one launch (start us, length us, event | category | flops | bytes accessed | tf_op | source)
XLA Modules:
  0.0 27.3 jit_solution(9454970465064310187)
XLA Ops:
  0.0 26.7 %sketch.1 = f32[1,64,128]{2,1,0:T(8,128)S(1)} custom-call(s32[16]{0:T(128)} %row_blocks_in.1, s32[8]{0:T(128)} %col_blocks_in.1, s32[16,128]{1,0:T(8,128)} %bitcast.2, s32[8,128]{1,0:T(8,128)} %bitcast.3, bf16[1,1024,2048]{2,1,0:T(8,128)(2,1)} %grads.1, bf16[1,1024,1024]{2,1,0:T(8,128)(2,1)} %inputs.1), custom_call_target="tpu_custom_call" | custom-call | tf_op jit(solution)/shard_map/sketch/pallas_call | solution.py:315
  26.7 0.6 %copy.8 = f32[1,64,128]{2,1,0:T(8,128)} copy(f32[1,64,128]{2,1,0:T(8,128)S(1)} %sketch.1) | data formatting | bytes 65536

commit v8 on v6

--- a/solution.py
+++ b/solution.py
@@ -211,10 +211,8 @@
             send(asum.at[chunk, (zh + step) % 4], zrecv.at[chunk, step - 1], zr.at[chunk], at_zh(step))
 
     def spread(chunk):
-        for step in (2, 1, 3):
-            for flip in range(2):
-                send(aall.at[col, chunk], aall.at[col, chunk], yr.at[chunk], at_col(step, flip))
-        send(aall.at[col, chunk], aall.at[col, chunk], yr.at[chunk], at_col(0, 1))
+        for step, flip in ((2, 1), (2, 0), (1, 1), (3, 1), (1, 0), (3, 0), (0, 1)):
+            send(aall.at[col, chunk], aall.at[col, chunk], yr.at[chunk], at_col(step, flip))
 
     def reduce_zh(chunk):
         arrived(zrecv.at[chunk], zr.at[chunk])

time: 27.4 us -> 27.3 us (level)
  no operation moved by 1% of the time
where the time goes in v8:
time: 27.3 us
  Pallas kernels  26.6 us (97%)
  local copies, waits for them, and re-layouts  0.62 us (2%)
    pallas_call x1, Pallas kernels, body(): pl.pallas_call(kernel, out_shape=pltpu.VMEM((1, 64, 128), F32), in_specs=...  26.6 us
    unnamed x1, local copies, waits for them, and re-layouts  0.62 us

profile of v8, /device:TPU:1, one launch (start us, length us, event | category | flops | bytes accessed | tf_op | source)
XLA Modules:
  0.0 27.3 jit_solution(14147944544725840250)
XLA Ops:
  0.0 26.6 %sketch.1 = f32[1,64,128]{2,1,0:T(8,128)S(1)} custom-call(s32[16]{0:T(128)} %row_blocks_in.1, s32[8]{0:T(128)} %col_blocks_in.1, s32[16,128]{1,0:T(8,128)} %bitcast.2, s32[8,128]{1,0:T(8,128)} %bitcast.3, bf16[1,1024,2048]{2,1,0:T(8,128)(2,1)} %grads.1, bf16[1,1024,1024]{2,1,0:T(8,128)(2,1)} %inputs.1), custom_call_target="tpu_custom_call" | custom-call | tf_op jit(solution)/shard_map/sketch/pallas_call | solution.py:313
  26.6 0.6 %copy.8 = f32[1,64,128]{2,1,0:T(8,128)} copy(f32[1,64,128]{2,1,0:T(8,128)S(1)} %sketch.1) | data formatting | bytes 65536

commit v9 on v8

--- a/solution.py
+++ b/solution.py
@@ -74,13 +74,6 @@
         return {"col": ((y + dy) % 4) * 2 + (core + dc) % 2}
 
     other_seq = {"seq": 1 - seq}
-
-    barrier = pltpu.get_barrier_semaphore()
-    partners = [at_x(step) for step in (2, 1, 3)]
-    partners += [at_col(step, flip) for step in (2, 1, 3) for flip in range(2)]
-    partners += [at_zh(1), at_zh(3), at_col(0, 1), other_seq]
-    for partner in partners:
-        pl.semaphore_signal(barrier, inc=1, device_id=partner, device_id_type=MESH)
 
     small = [
         pltpu.make_async_copy(src, dst, load_s.at[at])
@@ -103,7 +96,17 @@
         for chunk in range(CHUNKS)
         for half in range(2)
     ]
-    for load in loads_x[:1] + small[:2] + loads_x[1:2] + small[2:] + loads_y[:2] + loads_x[2:] + loads_y[2:]:
+    loads_x[0].start()
+    small[0].start()
+
+    barrier = pltpu.get_barrier_semaphore()
+    partners = [at_x(step) for step in (2, 1, 3)]
+    partners += [at_col(step, flip) for step in (2, 1, 3) for flip in range(2)]
+    partners += [at_zh(1), at_zh(3), at_col(0, 1), other_seq]
+    for partner in partners:
+        pl.semaphore_signal(barrier, inc=1, device_id=partner, device_id_type=MESH)
+
+    for load in small[1:2] + loads_x[1:2] + small[2:] + loads_y[:2] + loads_x[2:] + loads_y[2:]:
         load.start()
 
     def send(src, dst, recv_sem, device):

time: 27.3 us -> 27.4 us (level)
  no operation moved by 1% of the time
where the time goes in v9:
time: 27.4 us; the launch traced here: 27.3 us
  Pallas kernels  26.6 us (97%)
  local copies, waits for them, and re-layouts  0.62 us (2%)
    pallas_call x1, Pallas kernels, body(): pl.pallas_call(kernel, out_shape=pltpu.VMEM((1, 64, 128), F32), in_specs=...  26.6 us
    unnamed x1, local copies, waits for them, and re-layouts  0.62 us

profile of v9, /device:TPU:1, one launch (start us, length us, event | category | flops | bytes accessed | tf_op | source)
XLA Modules:
  0.0 27.3 jit_solution(6163206344221051460)
XLA Ops:
  0.0 26.6 %sketch.1 = f32[1,64,128]{2,1,0:T(8,128)S(1)} custom-call(s32[16]{0:T(128)} %row_blocks_in.1, s32[8]{0:T(128)} %col_blocks_in.1, s32[16,128]{1,0:T(8,128)} %bitcast.2, s32[8,128]{1,0:T(8,128)} %bitcast.3, bf16[1,1024,2048]{2,1,0:T(8,128)(2,1)} %grads.1, bf16[1,1024,1024]{2,1,0:T(8,128)(2,1)} %inputs.1), custom_call_target="tpu_custom_call" | custom-call | tf_op jit(solution)/shard_map/sketch/pallas_call | solution.py:316
  26.7 0.6 %copy.8 = f32[1,64,128]{2,1,0:T(8,128)} copy(f32[1,64,128]{2,1,0:T(8,128)S(1)} %sketch.1) | data formatting | bytes 65536
